TPU v7x, 32 devices: a whole 2x2x4 slice. The times are simulated.
32 devices in a mesh: dp: 16 (over z, y, core), tensor: 2 (over x).
Axes of the slice: x: 2, y: 2, z: 4, core: 2. Of those that a mesh axis runs over, the one named last changes fastest.
Arguments:
- tokens: bfloat16 [32768, 1024], P(('dp', 'tensor')), may hold values from -6 to 6
- gain_one: float32 [1024], replicated, may hold values from 0.5 to 1.5
- gain_two: float32 [1024], replicated, may hold values from 0.5 to 1.5
- w_query: bfloat16 [1024, 1024], P(None, 'tensor'), may hold values from -0.1875 to 0.1875
- w_key: bfloat16 [512, 1024], P('tensor'), may hold values from -0.1875 to 0.1875
- w_value: bfloat16 [512, 1024], P('tensor'), may hold values from -0.1875 to 0.1875
- w_out: bfloat16 [1024, 1024], P('tensor'), may hold values from -1 to 1
- w_gate: bfloat16 [32, 512, 1024], P(None, 'tensor'), may hold values from -0.1875 to 0.1875
- w_up: bfloat16 [32, 512, 1024], P(None, 'tensor'), may hold values from -0.1875 to 0.1875
- w_down: bfloat16 [32, 512, 1024], P(None, 'tensor'), may hold values from -1 to 1
- slot_index: int32 [16, 32, 640], P('dp'), may hold values from 0 to 2047, as said below
- slot_gate: float32 [16, 32, 640], P('dp'), may hold values from 0 to 0.19, as said below
- grad_output: bfloat16 [32768, 1024], P(('dp', 'tensor')), may hold values from -6 to 6
Outputs:
- output: bfloat16 [32768, 1024], P(('dp', 'tensor'))
- grad_tokens: bfloat16 [32768, 1024], P('dp')
- grad_gain_one: float32 [1024], replicated
- grad_gain_two: float32 [1024], replicated
- grad_w_query: float32 [1024, 1024], P(None, 'tensor')
- grad_w_key: float32 [512, 1024], P('tensor')
- grad_w_value: float32 [512, 1024], P('tensor')
- grad_w_out: float32 [1024, 1024], P('tensor')
- grad_w_gate: float32 [32, 512, 1024], P(None, 'tensor')
- grad_w_up: float32 [32, 512, 1024], P(None, 'tensor')
- grad_w_down: float32 [32, 512, 1024], P(None, 'tensor')
Inputs may be any that keep to these rules, and one draw needn't show every extreme that they name: `slot_index`: in each sequence group the 640 slots of one expert name distinct tokens of that group. `slot_gate`: in each expert's block the live slots (gate above zero) come first, followed by empty slots of gate zero; a block has 320 to 640 live slots, and in every sequence group some block is full.
All inputs are finite; a program needn't handle non-finite values.
Results may differ from a plain program's by a relative error of at most 0.023.
Values may be sent and summed in bfloat16 or wider, within the bound.
No kernel may reach another device: no remote copies, remote signals or barrier semaphores. Data moves between devices by JAX's collectives and lax.ppermute only.
A program may use at most 448 MiB of HBM per device.

v0:
```python
import math
import jax
import jax.numpy as jnp
from jax import lax
from jax.sharding import PartitionSpec as P

HD = 64
SEQ_LEN = 1024
EPS = 1e-05
THETA = 10000.0
MASKED = -1e30


def rope_tables(row_count, head_size):
    position = (jnp.arange(row_count) % SEQ_LEN).astype(jnp.float32)
    exponent = jnp.arange(head_size // 2).astype(jnp.float32) * (2.0 / head_size)
    angles = position[:, None] * jnp.power(THETA, -exponent)[None, :]
    return (jnp.cos(angles)[:, None, :], jnp.sin(angles)[:, None, :])


def rotate(values, cosine, sine_tab):
    half_size = values.shape[-1] // 2
    first, second = (values[..., :half_size], values[..., half_size:])
    return jnp.concatenate(
        [first * cosine - second * sine_tab, second * cosine + first * sine_tab], axis=-1
    )


def unrotate(grads_in, cosine, sine_tab):
    half_size = grads_in.shape[-1] // 2
    first, second = (grads_in[..., :half_size], grads_in[..., half_size:])
    return jnp.concatenate(
        [first * cosine + second * sine_tab, second * cosine - first * sine_tab], axis=-1
    )


def normalize(values, gain):
    inverse = lax.rsqrt(jnp.mean(values * values, axis=-1, keepdims=True) + EPS)
    return (values * inverse * gain, inverse)


def norm_back(values, inverse, gain, grad_normed):
    scaled = grad_normed * gain
    return inverse * scaled - values * inverse**3 * jnp.mean(
        scaled * values, axis=-1, keepdims=True
    )


def causal_mask(length):
    query_pos = lax.broadcasted_iota(jnp.int32, (length, length), 0)
    key_pos = lax.broadcasted_iota(jnp.int32, (length, length), 1)
    return key_pos <= query_pos


def attend_forward(members):
    queries, keys, values = members
    score_scale = queries.shape[-1] ** (-0.5)
    scores = (
        jnp.einsum("qgrd,kgd->grqk", queries, keys, preferred_element_type=jnp.float32)
        * score_scale
    )
    scores = jnp.where(causal_mask(queries.shape[0]), scores, MASKED)
    row_peak = jnp.max(scores, axis=-1, keepdims=True)
    exponent = jnp.exp(scores - row_peak)
    row_total = jnp.sum(exponent, axis=-1, keepdims=True)
    weights = (exponent / row_total).astype(jnp.bfloat16)
    mixed = jnp.einsum(
        "grqk,kgd->qgrd", weights, values, preferred_element_type=jnp.float32
    ).astype(jnp.bfloat16)
    return (mixed, row_peak[..., 0] + jnp.log(row_total[..., 0]))


def attend_backward(members):
    queries, keys, values, grad_mixed, log_total = members
    score_scale = queries.shape[-1] ** (-0.5)
    scores = (
        jnp.einsum("qgrd,kgd->grqk", queries, keys, preferred_element_type=jnp.float32)
        * score_scale
    )
    scores = jnp.where(causal_mask(queries.shape[0]), scores, MASKED)
    weights = jnp.exp(scores - log_total[..., None])
    grad_weights = jnp.einsum(
        "qgrd,kgd->grqk", grad_mixed, values, preferred_element_type=jnp.float32
    )
    grad_values = jnp.einsum(
        "grqk,qgrd->kgd",
        weights.astype(jnp.bfloat16),
        grad_mixed,
        preferred_element_type=jnp.float32,
    )
    row_delta = jnp.sum(grad_weights * weights, axis=-1, keepdims=True)
    grad_scores = (weights * (grad_weights - row_delta)).astype(jnp.bfloat16)
    grad_queries = (
        jnp.einsum("grqk,kgd->qgrd", grad_scores, keys, preferred_element_type=jnp.float32)
        * score_scale
    )
    grad_keys = (
        jnp.einsum("grqk,qgrd->kgd", grad_scores, queries, preferred_element_type=jnp.float32)
        * score_scale
    )
    return (grad_queries, grad_keys, grad_values)


def per_device(
    tokens,
    gain_one,
    gain_two,
    w_query,
    w_key,
    w_value,
    w_out,
    w_gate,
    w_up,
    w_down,
    slot_index,
    slot_gate,
    grad_output,
):
    n_tensor = lax.axis_size("tensor")
    shard_rows, width = tokens.shape
    head_size = HD
    local_heads = w_query.shape[1] // head_size
    local_groups = w_key.shape[0] // head_size
    expert_count, hidden_local, _ = w_gate.shape
    sweeps = math.gcd(expert_count, 4)
    slot_rows = slot_index[0].reshape(sweeps, expert_count // sweeps, -1)
    slot_weight = slot_gate[0].reshape(sweeps, expert_count // sweeps, -1)
    gate_blocks = w_gate.reshape(sweeps, expert_count // sweeps, hidden_local, width)
    up_blocks = w_up.reshape(sweeps, expert_count // sweeps, hidden_local, width)
    down_blocks = w_down.reshape(sweeps, expert_count // sweeps, hidden_local, width)
    row_start = lax.axis_index("tensor") * shard_rows
    full_rows = lax.all_gather(tokens, "tensor", axis=0, tiled=True)
    row_count = full_rows.shape[0]
    seq_count = row_count // SEQ_LEN
    cosine, sine_tab = rope_tables(row_count, head_size)
    rows_float = full_rows.astype(jnp.float32)
    normed_one, inverse_one = normalize(rows_float, gain_one)
    normed_one = normed_one.astype(jnp.bfloat16)
    query_pre = jnp.dot(normed_one, w_query, preferred_element_type=jnp.float32)
    key_pre = jnp.einsum("td,kd->tk", normed_one, w_key, preferred_element_type=jnp.float32)
    values = jnp.einsum(
        "td,kd->tk", normed_one, w_value, preferred_element_type=jnp.float32
    ).astype(jnp.bfloat16)
    queries = rotate(query_pre.reshape(row_count, local_heads, head_size), cosine, sine_tab).astype(
        jnp.bfloat16
    )
    keys = rotate(key_pre.reshape(row_count, local_groups, head_size), cosine, sine_tab).astype(
        jnp.bfloat16
    )
    seq_queries = queries.reshape(
        seq_count, SEQ_LEN, local_groups, local_heads // local_groups, head_size
    )
    seq_keys = keys.reshape(seq_count, SEQ_LEN, local_groups, head_size)
    seq_values = values.reshape(seq_count, SEQ_LEN, local_groups, head_size)
    mixed, log_total = lax.map(attend_forward, (seq_queries, seq_keys, seq_values))
    mixed = mixed.reshape(row_count, local_heads * head_size)
    attn_part = jnp.dot(mixed, w_out, preferred_element_type=jnp.float32)
    attn_shard = lax.psum_scatter(attn_part, "tensor", scatter_dimension=0, tiled=True)
    residual = tokens.astype(jnp.float32) + attn_shard
    normed_shard, inverse_two = normalize(residual, gain_two)
    normed_two = lax.all_gather(normed_shard.astype(jnp.bfloat16), "tensor", axis=0, tiled=True)

    def expert_forward(running, members):
        slot_part, weight_part, gate_part, up_part, down_part = members
        gathered = normed_two[slot_part]
        gate_pre = jnp.einsum(
            "ecd,efd->ecf", gathered, gate_part, preferred_element_type=jnp.float32
        )
        up_pre = jnp.einsum("ecd,efd->ecf", gathered, up_part, preferred_element_type=jnp.float32)
        active = (jax.nn.silu(gate_pre) * up_pre).astype(jnp.bfloat16)
        expert_out = (
            jnp.einsum("ecf,efd->ecd", active, down_part, preferred_element_type=jnp.float32)
            * weight_part[..., None]
        )
        running = running.at[slot_part.reshape(-1)].add(expert_out.reshape(-1, width))
        return (running, ())

    mixture_part, saved = lax.scan(
        expert_forward,
        jnp.zeros((row_count, width), jnp.float32),
        (slot_rows, slot_weight, gate_blocks, up_blocks, down_blocks),
    )
    mixture = lax.psum_scatter(
        mixture_part.astype(jnp.bfloat16), "tensor", scatter_dimension=0, tiled=True
    ).astype(jnp.float32)
    output = (residual + mixture).astype(jnp.bfloat16)
    grad_full = lax.all_gather(grad_output, "tensor", axis=0, tiled=True)

    def expert_backward(running, members):
        slot_part, weight_part, gate_part, up_part, down_part, kept_part = members
        gathered = normed_two[slot_part]
        gate_pre = jnp.einsum(
            "ecd,efd->ecf", gathered, gate_part, preferred_element_type=jnp.float32
        )
        up_pre = jnp.einsum("ecd,efd->ecf", gathered, up_part, preferred_element_type=jnp.float32)
        sigmoid_val = jax.nn.sigmoid(gate_pre)
        silu_val = gate_pre * sigmoid_val
        active = (silu_val * up_pre).astype(jnp.bfloat16)
        grad_out = (grad_full[slot_part].astype(jnp.float32) * weight_part[..., None]).astype(
            jnp.bfloat16
        )
        grad_act = jnp.einsum(
            "ecd,efd->ecf", grad_out, down_part, preferred_element_type=jnp.float32
        )
        grad_gate = (
            grad_act * up_pre * sigmoid_val * (1.0 + gate_pre * (1.0 - sigmoid_val))
        ).astype(jnp.bfloat16)
        grad_up = (grad_act * silu_val).astype(jnp.bfloat16)
        grad_down_w = jnp.einsum(
            "ecf,ecd->efd", active, grad_out, preferred_element_type=jnp.float32
        )
        grad_gate_w = jnp.einsum(
            "ecf,ecd->efd", grad_gate, gathered, preferred_element_type=jnp.float32
        )
        grad_up_w = jnp.einsum(
            "ecf,ecd->efd", grad_up, gathered, preferred_element_type=jnp.float32
        )
        grad_gathered = jnp.einsum(
            "ecf,efd->ecd", grad_gate, gate_part, preferred_element_type=jnp.float32
        )
        grad_gathered = grad_gathered + jnp.einsum(
            "ecf,efd->ecd", grad_up, up_part, preferred_element_type=jnp.float32
        )
        running = running.at[slot_part.reshape(-1)].add(grad_gathered.reshape(-1, width))
        grad_triple = (grad_gate_w, grad_up_w, grad_down_w)
        return (running, grad_triple)

    grad_normed_part, expert_grads = lax.scan(
        expert_backward,
        jnp.zeros((row_count, width), jnp.float32),
        (slot_rows, slot_weight, gate_blocks, up_blocks, down_blocks, saved),
    )
    grad_w_gate = expert_grads[0].reshape(expert_count, hidden_local, width)
    grad_w_up = expert_grads[1].reshape(expert_count, hidden_local, width)
    grad_w_down = expert_grads[2].reshape(expert_count, hidden_local, width)
    shared = (
        lax.psum_scatter(
            grad_w_gate.astype(jnp.bfloat16), "dp", scatter_dimension=2, tiled=True
        ).astype(jnp.float32),
        lax.psum_scatter(
            grad_w_up.astype(jnp.bfloat16), "dp", scatter_dimension=2, tiled=True
        ).astype(jnp.float32),
        lax.psum_scatter(
            grad_w_down.astype(jnp.bfloat16), "dp", scatter_dimension=2, tiled=True
        ).astype(jnp.float32),
    )
    grad_w_gate, grad_w_up, grad_w_down = (
        lax.all_gather(shared[0].astype(jnp.bfloat16), "dp", axis=2, tiled=True).astype(
            jnp.float32
        ),
        lax.all_gather(shared[1].astype(jnp.bfloat16), "dp", axis=2, tiled=True).astype(
            jnp.float32
        ),
        lax.all_gather(shared[2].astype(jnp.bfloat16), "dp", axis=2, tiled=True).astype(
            jnp.float32
        ),
    )
    grad_normed_two = lax.psum_scatter(
        grad_normed_part.astype(jnp.bfloat16), "tensor", scatter_dimension=0, tiled=True
    ).astype(jnp.float32)
    gain_two_part = jnp.sum(grad_normed_two * residual * inverse_two, axis=0)
    grad_resid = grad_output.astype(jnp.float32) + norm_back(
        residual, inverse_two, gain_two, grad_normed_two
    )
    grad_attn = lax.all_gather(grad_resid.astype(jnp.bfloat16), "tensor", axis=0, tiled=True)
    grad_w_out = jnp.dot(mixed.T, grad_attn, preferred_element_type=jnp.float32)
    grad_mixed = jnp.dot(grad_attn, w_out.T, preferred_element_type=jnp.float32).astype(
        jnp.bfloat16
    )
    grad_mixed = grad_mixed.reshape(
        seq_count, SEQ_LEN, local_groups, local_heads // local_groups, head_size
    )
    grad_q_rot, grad_k_rot, grad_v_seq = lax.map(
        attend_backward, (seq_queries, seq_keys, seq_values, grad_mixed, log_total)
    )
    grad_q = unrotate(grad_q_rot.reshape(row_count, local_heads, head_size), cosine, sine_tab)
    grad_q = grad_q.reshape(row_count, local_heads * head_size).astype(jnp.bfloat16)
    grad_k = unrotate(grad_k_rot.reshape(row_count, local_groups, head_size), cosine, sine_tab)
    grad_k = grad_k.reshape(row_count, local_groups * head_size).astype(jnp.bfloat16)
    grad_v = grad_v_seq.reshape(row_count, local_groups * head_size).astype(jnp.bfloat16)
    grad_w_query = jnp.dot(normed_one.T, grad_q, preferred_element_type=jnp.float32)
    grad_w_key = jnp.dot(grad_k.T, normed_one, preferred_element_type=jnp.float32)
    grad_w_value = jnp.dot(grad_v.T, normed_one, preferred_element_type=jnp.float32)
    grad_normed_one = jnp.dot(grad_q, w_query.T, preferred_element_type=jnp.float32)
    grad_normed_one = grad_normed_one + jnp.dot(grad_k, w_key, preferred_element_type=jnp.float32)
    grad_normed_one = grad_normed_one + jnp.dot(grad_v, w_value, preferred_element_type=jnp.float32)
    gain_one_part = jnp.sum(grad_normed_one * rows_float * inverse_one, axis=0)
    gains_tile = jnp.broadcast_to(
        jnp.stack([gain_one_part, gain_two_part])[None], (n_tensor, 2, width)
    )
    grad_normed_shard, gains_sum = (
        lax.psum_scatter(
            grad_normed_one.astype(jnp.bfloat16), "tensor", scatter_dimension=0, tiled=True
        ).astype(jnp.float32),
        lax.psum_scatter(
            gains_tile.astype(jnp.bfloat16), "tensor", scatter_dimension=0, tiled=True
        ).astype(jnp.float32),
    )
    inverse_shard = lax.dynamic_slice_in_dim(inverse_one, row_start, shard_rows, 0)
    grad_input = grad_resid + norm_back(
        tokens.astype(jnp.float32), inverse_shard, gain_one, grad_normed_shard
    )
    grad_tokens = lax.all_gather(grad_input.astype(jnp.bfloat16), "tensor", axis=0, tiled=True)
    grad_w_query, grad_w_key, grad_w_value, grad_w_out, gains_total = (
        lax.psum(grad_w_query.astype(jnp.bfloat16), "dp").astype(jnp.float32),
        lax.psum(grad_w_key.astype(jnp.bfloat16), "dp").astype(jnp.float32),
        lax.psum(grad_w_value.astype(jnp.bfloat16), "dp").astype(jnp.float32),
        lax.psum(grad_w_out.astype(jnp.bfloat16), "dp").astype(jnp.float32),
        lax.psum(gains_sum.astype(jnp.bfloat16), "dp").astype(jnp.float32),
    )
    return (
        output,
        grad_tokens,
        gains_total[0, 0],
        gains_total[0, 1],
        grad_w_query,
        grad_w_key,
        grad_w_value,
        grad_w_out,
        grad_w_gate,
        grad_w_up,
        grad_w_down,
    )


def solution(mesh):
    placed = (
        P(("dp", "tensor"), None),
        P(),
        P(),
        P(None, "tensor"),
        P("tensor", None),
        P("tensor", None),
        P("tensor", None),
        P(None, "tensor", None),
        P(None, "tensor", None),
        P(None, "tensor", None),
        P("dp", None, None),
        P("dp", None, None),
        P(("dp", "tensor"), None),
    )
    return jax.shard_map(
        per_device,
        mesh=mesh,
        in_specs=placed,
        out_specs=(
            P(("dp", "tensor"), None),
            P("dp", None),
            P(),
            P(),
            P(None, "tensor"),
            P("tensor", None),
            P("tensor", None),
            P("tensor", None),
            P(None, "tensor", None),
            P(None, "tensor", None),
            P(None, "tensor", None),
        ),
        check_vma=False,
    )
```

profile of v0, /device:TPU:0, one launch (start us, length us, event | category | flops | bytes accessed | tf_op | source)
XLA Modules:
  0.0 3397.9 jit_solution(16931180885736290006)
XLA Ops:
  9.8 59.3 %all-gather.9.cloned.1.call-done = bf16[2048,1024]{1,0:T(8,128)(2,1)} async-done(((bf16[1024,1024]{1,0:T(8,128)(2,1)}), bf16[2048,1024]{1,0:T(8,128)(2,1)}) %all-gather.9.cloned.1.call-update) | async-done | bytes 4194320 | tf_op jit(solution)/shard_map/all_gather | solution.py:132
  109.0 92.2 %while.52 = (s32[]{:T(128)}, bf16[2,1024,4,2,64]{1,4,3,2,0:T(8,128)(2,1)S(1)}, f32[2,4,2,1024]{3,2,1,0:T(2,128)S(1)}, bf16[2,1024,4,64]{1,3,2,0:T(8,128)(2,1)}, ...) while((s32[]{:T(128)}, bf16[2,1024,4,2,64]{1,4,3,2,0:T(8,128)(2,1)S(1)}, ...), condition=%wide.region_4.5_spmd, body=%wide.region_1.4_spmd.sunk | while | flops 2249711616 | bytes 108267600 | solution.py:155
  211.9 98.6 %reduce-scatter.8.cloned.1.call-done = f32[1024,1024]{1,0:T(8,128)} async-done(((f32[2048,1024]{1,0:T(8,128)}), f32[1024,1024]{1,0:T(8,128)}) %reduce-scatter.8.cloned.1.call-update) | async-done | bytes 4194320 | tf_op jit(solution)/shard_map/reduce_scatter | solution.py:158
  317.2 51.8 %all-gather.13.cloned.1.call-done = bf16[2048,1024]{1,0:T(8,128)(2,1)} async-done(((bf16[1024,1024]{1,0:T(8,128)(2,1)}), bf16[2048,1024]{1,0:T(8,128)(2,1)}) %all-gather.13.cloned.1.call-update) | async-done | bytes 4194320 | tf_op jit(solution)/shard_map/all_gather | solution.py:187
  368.9 58.8 %all-gather.11.cloned.1.call-done = bf16[2048,1024]{1,0:T(8,128)(2,1)} async-done(((bf16[1024,1024]{1,0:T(8,128)(2,1)}), bf16[2048,1024]{1,0:T(8,128)(2,1)}) %all-gather.11.cloned.1.call-update) | async-done | bytes 4194320 | tf_op jit(solution)/shard_map/all_gather | solution.py:161
  432.2 820.3 %while.54 = (s32[]{:T(128)}, f32[2048,1024]{1,0:T(8,128)}, bf16[4,8,256,1024]{3,2,1,0:T(8,128)(2,1)}, bf16[4,8,256,1024]{3,2,1,0:T(8,128)(2,1)}, bf16[4,8,256,10...) while((s32[]{:T(128)}, f32[2048,1024]{1,0:T(8,128)}, ...), condition=%wide.region_13.14_spmd, body=%wide.region_11.13_spmd.sunk | while | flops 21541720064 | bytes 387395840 | solution.py:228
  435.2 28.4 gather_fusion.2
  463.6 28.4 gather_fusion.1
  585.8 51.6 %scatter_fusion.1 = f32[2048,1024]{1,0:T(8,128)} fusion(f32[2048,1024]{1,0:T(8,128)} %get-tuple-element.630, s32[5120]{0:T(1024)S(1)} %bitcast.412, f32[5120,1024]{1,0:T(8,128)} %bitcast.389), kind=kCustom, calls=%fused_computation.4.clone.1 | custom fusion | flops 5242880 | bytes 62935040 | tf_op jit(solution)/shard_map/while/body/eval_jaxpr/scatter-add | solution.py:224
  640.2 28.4 gather_fusion.2
  668.7 28.4 gather_fusion.1
  790.7 51.6 %scatter_fusion.1 = f32[2048,1024]{1,0:T(8,128)} fusion(f32[2048,1024]{1,0:T(8,128)} %get-tuple-element.630, s32[5120]{0:T(1024)S(1)} %bitcast.412, f32[5120,1024]{1,0:T(8,128)} %bitcast.389), kind=kCustom, calls=%fused_computation.4.clone.1 | custom fusion | flops 5242880 | bytes 62935040 | tf_op jit(solution)/shard_map/while/body/eval_jaxpr/scatter-add | solution.py:224
  845.1 28.4 gather_fusion.2
  873.5 28.4 gather_fusion.1
  995.6 51.6 %scatter_fusion.1 = f32[2048,1024]{1,0:T(8,128)} fusion(f32[2048,1024]{1,0:T(8,128)} %get-tuple-element.630, s32[5120]{0:T(1024)S(1)} %bitcast.412, f32[5120,1024]{1,0:T(8,128)} %bitcast.389), kind=kCustom, calls=%fused_computation.4.clone.1 | custom fusion | flops 5242880 | bytes 62935040 | tf_op jit(solution)/shard_map/while/body/eval_jaxpr/scatter-add | solution.py:224
  1050.1 28.4 gather_fusion.2
  1078.5 28.4 gather_fusion.1
  1200.5 51.6 %scatter_fusion.1 = f32[2048,1024]{1,0:T(8,128)} fusion(f32[2048,1024]{1,0:T(8,128)} %get-tuple-element.630, s32[5120]{0:T(1024)S(1)} %bitcast.412, f32[5120,1024]{1,0:T(8,128)} %bitcast.389), kind=kCustom, calls=%fused_computation.4.clone.1 | custom fusion | flops 5242880 | bytes 62935040 | tf_op jit(solution)/shard_map/while/body/eval_jaxpr/scatter-add | solution.py:224
  1258.6 54.4 %reduce-scatter.12.cloned.1.call-done = bf16[1024,1024]{1,0:T(8,128)(2,1)} async-done(((bf16[2048,1024]{1,0:T(8,128)(2,1)}), bf16[1024,1024]{1,0:T(8,128)(2,1)}) %reduce-scatter.12.cloned.1.call-update) | async-done | bytes 2097168 | tf_op jit(solution)/shard_map/reduce_scatter | solution.py:258
  1322.2 56.8 %all-gather.15.cloned.1.call-done = bf16[2048,1024]{1,0:T(8,128)(2,1)} async-done(((bf16[1024,1024]{1,0:T(8,128)(2,1)}), bf16[2048,1024]{1,0:T(8,128)(2,1)}) %all-gather.15.cloned.1.call-update) | async-done | bytes 4194320 | tf_op jit(solution)/shard_map/all_gather | solution.py:265
  1397.8 333.4 %while.55 = (s32[]{:T(128)}, f32[2,1024,4,2,64]{1,0,4,3,2:T(2,128)}, f32[2,1024,4,64]{1,0,3,2:T(2,128)}, bf16[2,1024,4,64]{1,3,2,0:T(8,128)(2,1)}, bf16[2,1024,4...) while((s32[]{:T(128)}, ...), condition=%wide.region_18.19_spmd, body=%wide.region_16.18_spmd.sunk | while | flops 5496365056 | bytes 282823840 | solution.py:273
  1431.6 24.7 fusion.240
  1456.4 28.1 fusion.241
  1527.8 36.6 %dynamic_update_slice.49 = f32[2,1024,4,2,64]{1,0,4,3,2:T(2,128)} dynamic-update-slice(f32[2,1024,4,2,64]{1,0,4,3,2:T(2,128)} %get-tuple-element.667, f32[1,1024,4,2,64]{1,0,4,3,2:T(1,128)S(1)} %copy.117, s32[]{:T(128)S(6)} %copy.157, s32[]{:T(128)} %constant.123.clone.1..sunk, s32[]{:T(128)} %constant.123.clone.1..sunk, s32[]{:T(128)} %constant.123.clone.1..sunk, s32[]{:T(128)} %constant.123.clone.1..sunk) | dynamic-update-slice | bytes 4194308 | tf_op jit(solution)/shard_map/while/body/jit(dynamic_update_index_in_dim)/dynamic_update_slice | solution.py:273
  1598.1 24.7 fusion.240
  1622.8 28.1 fusion.241
  1694.2 36.6 %dynamic_update_slice.49 = f32[2,1024,4,2,64]{1,0,4,3,2:T(2,128)} dynamic-update-slice(f32[2,1024,4,2,64]{1,0,4,3,2:T(2,128)} %get-tuple-element.667, f32[1,1024,4,2,64]{1,0,4,3,2:T(1,128)S(1)} %copy.117, s32[]{:T(128)S(6)} %copy.157, s32[]{:T(128)} %constant.123.clone.1..sunk, s32[]{:T(128)} %constant.123.clone.1..sunk, s32[]{:T(128)} %constant.123.clone.1..sunk, s32[]{:T(128)} %constant.123.clone.1..sunk) | dynamic-update-slice | bytes 4194308 | tf_op jit(solution)/shard_map/while/body/jit(dynamic_update_index_in_dim)/dynamic_update_slice | solution.py:273
  1769.2 432.4 %while.53 = (s32[]{:T(128)}, f32[2048,1024]{1,0:T(8,128)}, s32[4,8,640]{2,1,0:T(8,128)}, bf16[2048,1024]{1,0:T(8,128)(2,1)}, bf16[4,8,256,1024]{3,2,1,0:T(8,128)...) while((s32[]{:T(128)}, f32[2048,1024]{1,0:T(8,128)}, ...), condition=%wide.region_9.10_spmd, body=%wide.region_7.9_spmd.sunk | while | flops 8071449600 | bytes 149247088 | solution.py:178
  1771.7 28.4 gather_fusion
  1826.0 51.6 %scatter_fusion = f32[2048,1024]{1,0:T(8,128)} fusion(f32[2048,1024]{1,0:T(8,128)} %get-tuple-element.698, s32[5120]{0:T(1024)S(1)} %bitcast.413, f32[5120,1024]{1,0:T(8,128)} %bitcast.390), kind=kCustom, calls=%fused_computation.3.clone.1 | custom fusion | flops 5242880 | bytes 62935040 | tf_op jit(solution)/shard_map/while/body/eval_jaxpr/scatter-add | solution.py:175
  1879.8 28.4 gather_fusion
  1933.9 51.6 %scatter_fusion = f32[2048,1024]{1,0:T(8,128)} fusion(f32[2048,1024]{1,0:T(8,128)} %get-tuple-element.698, s32[5120]{0:T(1024)S(1)} %bitcast.413, f32[5120,1024]{1,0:T(8,128)} %bitcast.390), kind=kCustom, calls=%fused_computation.3.clone.1 | custom fusion | flops 5242880 | bytes 62935040 | tf_op jit(solution)/shard_map/while/body/eval_jaxpr/scatter-add | solution.py:175
  1987.8 28.4 gather_fusion
  2041.9 51.6 %scatter_fusion = f32[2048,1024]{1,0:T(8,128)} fusion(f32[2048,1024]{1,0:T(8,128)} %get-tuple-element.698, s32[5120]{0:T(1024)S(1)} %bitcast.413, f32[5120,1024]{1,0:T(8,128)} %bitcast.390), kind=kCustom, calls=%fused_computation.3.clone.1 | custom fusion | flops 5242880 | bytes 62935040 | tf_op jit(solution)/shard_map/while/body/eval_jaxpr/scatter-add | solution.py:175
  2095.8 28.4 gather_fusion
  2150.0 51.6 %scatter_fusion = f32[2048,1024]{1,0:T(8,128)} fusion(f32[2048,1024]{1,0:T(8,128)} %get-tuple-element.698, s32[5120]{0:T(1024)S(1)} %bitcast.413, f32[5120,1024]{1,0:T(8,128)} %bitcast.390), kind=kCustom, calls=%fused_computation.3.clone.1 | custom fusion | flops 5242880 | bytes 62935040 | tf_op jit(solution)/shard_map/while/body/eval_jaxpr/scatter-add | solution.py:175
  2310.2 135.2 %reduce-scatter.20.cloned.1.call-done = bf16[32,256,64]{1,0,2:T(8,128)(2,1)} async-done(((bf16[32,256,1024]{1,0,2:T(8,128)(2,1)}), bf16[32,256,64]{1,0,2:T(8,128)(2,1)}) %reduce-scatter.20.cloned.1.call-update) | async-done | bytes 1048592 | tf_op jit(solution)/shard_map/reduce_scatter | solution.py:243
  2445.4 182.1 %reduce-scatter.16.cloned.1.call-done = bf16[32,256,64]{1,0,2:T(8,128)(2,1)} async-done(((bf16[32,256,1024]{1,0,2:T(8,128)(2,1)}), bf16[32,256,64]{1,0,2:T(8,128)(2,1)}) %reduce-scatter.16.cloned.1.call-update) | async-done | bytes 1048592 | tf_op jit(solution)/shard_map/reduce_scatter | solution.py:237
  2627.6 182.2 %reduce-scatter.18.cloned.1.call-done = bf16[32,256,64]{1,0,2:T(8,128)(2,1)} async-done(((bf16[32,256,1024]{1,0,2:T(8,128)(2,1)}), bf16[32,256,64]{1,0,2:T(8,128)(2,1)}) %reduce-scatter.18.cloned.1.call-update) | async-done | bytes 1048592 | tf_op jit(solution)/shard_map/reduce_scatter | solution.py:240
  2816.2 31.2 psum.35
  2848.0 69.6 %all-reduce.4.cloned.1.call-done = (bf16[1024,512]{1,0:T(8,128)(2,1)}, bf16[256,1024]{1,0:T(8,128)(2,1)}, bf16[256,1024]{1,0:T(8,128)(2,1)}, bf16[512,1024]{1,0:T(8,128)(2,1)}) async-done(((bf16[1024,512]{1,0:T(8,128)(2,1)}, bf16[256,1024]{1,0:T(8,128)(2,1)}, bf16[256,1024]{1,0:T(8,128)(2,1)}, bf16[512,1024]{1,0:T(8,128)(2,1)}), (bf16[1024,512]{1,0:T(8,128)(2,1)}, bf16[256,1024]{1,0:T(8,128)(2,1)}, ...) | async-done | bytes 3145744 | tf_op jit(solution)/shard_map/psum | solution.py:305
  2925.3 50.2 %all-gather.17.cloned.1.call-done = bf16[2048,1024]{1,0:T(8,128)(2,1)} async-done(((bf16[1024,1024]{1,0:T(8,128)(2,1)}), bf16[2048,1024]{1,0:T(8,128)(2,1)}) %all-gather.17.cloned.1.call-update) | async-done | bytes 4194320 | tf_op jit(solution)/shard_map/all_gather | solution.py:303
  2975.6 128.9 %all-gather.23.cloned.1.call-done = bf16[32,256,1024]{1,0,2:T(8,128)(2,1)} async-done(((bf16[32,256,64]{1,0,2:T(8,128)(2,1)}), bf16[32,256,1024]{1,0,2:T(8,128)(2,1)}) %all-gather.23.cloned.1.call-update) | async-done | bytes 16777232 | tf_op jit(solution)/shard_map/all_gather | solution.py:254
  3104.5 27.8 copy.79
  3132.3 99.4 %all-gather.19.cloned.1.call-done = bf16[32,256,1024]{1,0,2:T(8,128)(2,1)} async-done(((bf16[32,256,64]{1,0,2:T(8,128)(2,1)}), bf16[32,256,1024]{1,0,2:T(8,128)(2,1)}) %all-gather.19.cloned.1.call-update) | async-done | bytes 16777232 | tf_op jit(solution)/shard_map/all_gather | solution.py:248
  3231.6 27.8 copy.77
  3259.4 99.3 %all-gather.21.cloned.1.call-done = bf16[32,256,1024]{1,0,2:T(8,128)(2,1)} async-done(((bf16[32,256,64]{1,0,2:T(8,128)(2,1)}), bf16[32,256,1024]{1,0,2:T(8,128)(2,1)}) %all-gather.21.cloned.1.call-update) | async-done | bytes 16777232 | tf_op jit(solution)/shard_map/all_gather | solution.py:251
  3358.7 27.5 copy.78
  (383 shorter events, 1007.2 us)
Async XLA Ops:
  7.2 198.1 %copy-start = (bf16[512,1024]{1,0:T(8,128)(2,1)S(1)}, bf16[512,1024]{1,0:T(8,128)(2,1)}, u32[]{:S(2)}) copy-start(bf16[512,1024]{1,0:T(8,128)(2,1)} %param.27) | copy-start | bytes 3145732
  7.2 65.1 %copy-start.51 = (f32[1024]{0:T(1024)S(1)}, f32[1024]{0:T(1024)}, u32[]{:S(2)}) copy-start(f32[1024]{0:T(1024)} %param.22) | copy-start | bytes 12292
  7.2 61.9 %all-gather.9.cloned.1.call-start = ((), (), s32[]{:S(2)}) async-start(), calls=%async_computation.7 | async-start | bytes 6291456 | tf_op jit(solution)/shard_map/all_gather | solution.py:132
  7.9 302.6 %reduce-scatter.8.cloned.1.call-start = ((), (), s32[]{:S(2)}) async-start(), calls=%async_computation.8 | async-start | bytes 12582912 | tf_op jit(solution)/shard_map/reduce_scatter | solution.py:158
  9.8 88.0 %copy-start.13 = (f32[2048,32]{0,1:T(8,128)}, f32[2048,32]{0,1:T(8,128)S(1)}, u32[]{:S(2)}) copy-start(f32[2048,32]{0,1:T(8,128)S(1)} %get-tuple-element.362) | copy-start | bytes 786436
  211.1 99.4 %copy-start.10 = (bf16[1024,1024]{1,0:T(8,128)(2,1)S(1)}, bf16[1024,1024]{1,0:T(8,128)(2,1)}, u32[]{:S(2)}) copy-start(bf16[1024,1024]{1,0:T(8,128)(2,1)} %param.21) | copy-start | bytes 6291460
  211.1 157.8 %all-gather.13.cloned.1.call-start = ((), (), s32[]{:S(2)}) async-start(), calls=%async_computation.11 | async-start | bytes 6291456 | tf_op jit(solution)/shard_map/all_gather | solution.py:187
  211.9 103.5 %copy-start.44 = (f32[1024]{0:T(1024)S(1)}, f32[1024]{0:T(1024)}, u32[]{:S(2)}) copy-start(f32[1024]{0:T(1024)} %param.23) | copy-start | bytes 12292
  211.9 215.9 %all-gather.11.cloned.1.call-start = ((), (), s32[]{:S(2)}) async-start(), calls=%async_computation.9 | async-start | bytes 6291456 | tf_op jit(solution)/shard_map/all_gather | solution.py:161
  317.1 995.9 %reduce-scatter.12.cloned.1.call-start = ((), (), s32[]{:S(2)}) async-start(), calls=%async_computation.12 | async-start | bytes 6291456 | tf_op jit(solution)/shard_map/reduce_scatter | solution.py:258
  492.0 10.5 copy-start.2
  535.3 10.4 copy-start.4
  545.7 9.4 copy-start.3
  566.3 19.4 copy-start.30
  697.1 10.5 copy-start.2
  740.2 10.4 copy-start.4
  750.6 9.3 copy-start.3
  771.2 19.4 copy-start.30
  902.0 10.5 copy-start.2
  945.2 10.4 copy-start.4
  955.6 9.4 copy-start.3
  976.2 19.4 copy-start.30
  1107.0 10.5 copy-start.2
  1150.1 10.4 copy-start.4
  1160.4 9.3 copy-start.3
  1181.0 19.4 copy-start.30
  1258.5 54.5 %copy-start.39 = (f32[1024]{0:T(1024)S(1)}, f32[1024]{0:T(1024)}, u32[]{:S(2)}) copy-start(f32[1024]{0:T(1024)} %copy-done.38) | copy-start | bytes 12292
  1258.5 54.5 %copy-start.45 = (f32[1024]{0:T(1024)S(1)}, f32[1024]{0:T(1024)}, u32[]{:S(2)}) copy-start(f32[1024]{0:T(1024)} %param.23) | copy-start | bytes 12292
  1258.5 59.9 %copy-start.12 = (bf16[1024,1024]{1,0:T(8,128)(2,1)S(1)}, bf16[1024,1024]{1,0:T(8,128)(2,1)}, u32[]{:S(2)}) copy-start(bf16[1024,1024]{1,0:T(8,128)(2,1)} %param.33) | copy-start | bytes 6291460
  1258.6 59.9 %copy-start.47 = (f32[1024]{0:T(1024)S(1)}, f32[1024]{0:T(1024)}, u32[]{:S(2)}) copy-start(f32[1024]{0:T(1024)} %get-tuple-element.366) | copy-start | bytes 12292
  1258.6 120.4 %all-gather.15.cloned.1.call-start = ((), (), s32[]{:S(2)}) async-start(), calls=%async_computation.13 | async-start | bytes 6291456 | tf_op jit(solution)/shard_map/all_gather | solution.py:265
  1322.1 976.1 %reduce-scatter.14.cloned.1.call-start = ((), (), s32[]{:S(2)}) async-start(), calls=%async_computation.14 | async-start | bytes 6291456 | tf_op jit(solution)/shard_map/reduce_scatter | solution.py:292
  1387.1 10.6 copy-start.37
  1731.2 6.7 copy-start.14
  1764.8 537.2 %reduce-scatter.10.cloned.1.call-start = ((), (), s32[]{:S(2)}) async-start(), calls=%async_computation.10 | async-start | bytes 6291456 | tf_op jit(solution)/shard_map/reduce_scatter | solution.py:183
  2207.7 237.7 %reduce-scatter.20.cloned.1.call-start = ((), (), s32[]{:S(2)}) async-start(), calls=%async_computation.20 | async-start | bytes 17825792 | tf_op jit(solution)/shard_map/reduce_scatter | solution.py:243
  2231.8 395.7 %reduce-scatter.16.cloned.1.call-start = ((), (), s32[]{:S(2)}) async-start(), calls=%async_computation.16 | async-start | bytes 17825792 | tf_op jit(solution)/shard_map/reduce_scatter | solution.py:237
  2256.3 553.5 %reduce-scatter.18.cloned.1.call-start = ((), (), s32[]{:S(2)}) async-start(), calls=%async_computation.18 | async-start | bytes 17825792 | tf_op jit(solution)/shard_map/reduce_scatter | solution.py:240
  2280.9 7.7 copy-start.18
  2280.9 636.7 %all-reduce.4.cloned.1.call-start = ((), (), s32[]{:S(2)}) async-start(), calls=%async_computation.22 | async-start | bytes 6291456 | tf_op jit(solution)/shard_map/psum | solution.py:305
  2281.6 7.0 copy-start.22
  2298.1 677.4 %all-gather.17.cloned.1.call-start = ((), (), s32[]{:S(2)}) async-start(), calls=%async_computation.15 | async-start | bytes 6291456 | tf_op jit(solution)/shard_map/all_gather | solution.py:303
  2310.1 499.8 %copy-start.58 = (u32[32]{0:T(128)S(1)}, u32[32]{0:T(128)}, u32[]{:S(2)}) copy-start(u32[32]{0:T(128)} %constant.138) | copy-start | bytes 388
  2310.1 500.4 %copy-start.53 = (bf16[1024]{0:T(1024)(128)(2,1)S(1)}, bf16[1024]{0:T(1024)(128)(2,1)}, u32[]{:S(2)}) copy-start(bf16[1024]{0:T(1024)(128)(2,1)} %get-tuple-element.266) | copy-start | bytes 6148
  2310.1 500.4 %copy-start.54 = (bf16[1024]{0:T(1024)(128)(2,1)S(1)}, bf16[1024]{0:T(1024)(128)(2,1)}, u32[]{:S(2)}) copy-start(bf16[1024]{0:T(1024)(128)(2,1)} %get-tuple-element.350) | copy-start | bytes 6148
  2310.1 794.4 %all-gather.23.cloned.1.call-start = ((), (), s32[]{:S(2)}) async-start(), calls=%async_computation.21 | async-start | bytes 17825792 | tf_op jit(solution)/shard_map/all_gather | solution.py:254
  2445.4 786.2 %all-gather.19.cloned.1.call-start = ((), (), s32[]{:S(2)}) async-start(), calls=%async_computation.17 | async-start | bytes 17825792 | tf_op jit(solution)/shard_map/all_gather | solution.py:248
  2627.6 731.2 %all-gather.21.cloned.1.call-start = ((), (), s32[]{:S(2)}) async-start(), calls=%async_computation.19 | async-start | bytes 17825792 | tf_op jit(solution)/shard_map/all_gather | solution.py:251
  (40 other events, 131.8 us)
Sparse Core Ops, SparseCore 0:
  9.6 59.4 all-gather.8
  211.3 99.2 reduce-scatter.7
  312.2 56.7 all-gather.12
  371.0 56.7 all-gather.10
  1258.7 54.3 reduce-scatter.11
  1322.2 56.7 all-gather.14
  1764.9 54.2 reduce-scatter.13
  2207.8 54.7 reduce-scatter.9
  2266.7 178.6 reduce-scatter.19
  2449.9 177.5 reduce-scatter.15
  2632.2 177.5 reduce-scatter.17
  2814.7 102.8 all-reduce.3
  2919.7 55.7 all-gather.16
  2977.6 126.8 all-gather.22
  3106.5 125.0 all-gather.18
  3233.6 125.0 all-gather.20
where the time goes:
time: 3420 us; the launch traced here: 3400 us
  waiting for transfers between devices  1330 us (39%)
  matrix products  749 us (22%)
  local copies, waits for them, and re-layouts  697 us (20%)
  other arithmetic  570 us (17%)
  blocking collectives  36.2 us (1%)
    scatter-add x4, other arithmetic, expert_backward(): running.at[slot_part.reshape(-1)].add(grad_gathered.reshape(-1, width))  206 us
    scatter-add x4, other arithmetic, expert_forward(): running.at[slot_part.reshape(-1)].add(expert_out.reshape(-1, width))  206 us
    reduce_scatter x1, waiting for transfers between devices, per_device(): lax.psum_scatter(grad_w_up.astype(jnp.bfloat16), 'dp', scatter_dimension=...  182 us
    reduce_scatter x1, waiting for transfers between devices, per_device(): lax.psum_scatter(grad_w_gate.astype(jnp.bfloat16), 'dp', scatter_dimensio...  182 us
    reduce_scatter x1, waiting for transfers between devices, per_device(): lax.psum_scatter(grad_w_down.astype(jnp.bfloat16), 'dp', scatter_dimensio...  135 us
    all_gather x1, waiting for transfers between devices, per_device(): lax.all_gather(shared[2].astype(jnp.bfloat16), 'dp', axis=2, tiled=True)  129 us
    dynamic_update_slice x8, local copies, waits for them, and re-layouts, per_device(): lax.map(attend_backward, (seq_queries, seq_keys, seq_values, grad_mixed,...  117 us
    gather x4, local copies, waits for them, and re-layouts, expert_backward(): grad_full[slot_part].astype(jnp.float32) * weight_part[..., None]  114 us
  transfers between devices with their start and end apart: 16, of which 14 were waited for; matrix products, arithmetic and copies ran while one was open for 18% of the time, Pallas kernels for 0%

commit v1 on v0

--- a/solution.py
+++ b/solution.py
@@ -302,7 +302,9 @@
     )
     grad_tokens = lax.all_gather(grad_input.astype(jnp.bfloat16), "tensor", axis=0, tiled=True)
     grad_w_query, grad_w_key, grad_w_value, grad_w_out, gains_total = (
-        lax.psum(grad_w_query.astype(jnp.bfloat16), "dp").astype(jnp.float32),
+        jnp.sum(lax.all_gather(grad_w_query.astype(jnp.bfloat16), "dp"), axis=0).astype(
+            jnp.float32
+        ),
         lax.psum(grad_w_key.astype(jnp.bfloat16), "dp").astype(jnp.float32),
         lax.psum(grad_w_value.astype(jnp.bfloat16), "dp").astype(jnp.float32),
         lax.psum(grad_w_out.astype(jnp.bfloat16), "dp").astype(jnp.float32),

time: 3420 us -> 3540 us (1.035)
  waiting for transfers between devices: 1330 us -> 1440 us
    all_gather x0 -> x1, waiting for transfers between devices: none -> 130 us  [per_device(): lax.all_gather(grad_w_query.astype(jnp.bfloat16), 'dp')]
    unnamed x116 -> x110, local copies, waits for them, and re-layouts: 102 us -> 102 us
  transfers between devices with their start and end apart: 16 -> 17, of which waited for: 14 -> 15; matrix products, arithmetic and copies ran while one was open for 18% -> 18% of each run, Pallas kernels for 0% -> 0%
where the time goes in v1:
time: 3540 us; the launch traced here: 3520 us
  waiting for transfers between devices  1440 us (41%)
  matrix products  751 us (21%)
  local copies, waits for them, and re-layouts  697 us (20%)
  other arithmetic  580 us (16%)
  blocking collectives  36 us (1%)
    scatter-add x4, other arithmetic, expert_backward(): running.at[slot_part.reshape(-1)].add(grad_gathered.reshape(-1, width))  206 us
    scatter-add x4, other arithmetic, expert_forward(): running.at[slot_part.reshape(-1)].add(expert_out.reshape(-1, width))  206 us
    reduce_scatter x1, waiting for transfers between devices, per_device(): lax.psum_scatter(grad_w_up.astype(jnp.bfloat16), 'dp', scatter_dimension=...  182 us
    reduce_scatter x1, waiting for transfers between devices, per_device(): lax.psum_scatter(grad_w_gate.astype(jnp.bfloat16), 'dp', scatter_dimensio...  182 us
    reduce_scatter x1, waiting for transfers between devices, per_device(): lax.psum_scatter(grad_w_down.astype(jnp.bfloat16), 'dp', scatter_dimensio...  133 us
    all_gather x1, waiting for transfers between devices, per_device(): lax.all_gather(grad_w_query.astype(jnp.bfloat16), 'dp')  130 us
    dynamic_update_slice x8, local copies, waits for them, and re-layouts, per_device(): lax.map(attend_backward, (seq_queries, seq_keys, seq_values, grad_mixed,...  117 us
    all_gather x1, waiting for transfers between devices, per_device(): lax.all_gather(shared[2].astype(jnp.bfloat16), 'dp', axis=2, tiled=True)  116 us
  transfers between devices with their start and end apart: 17, of which 15 were waited for; matrix products, arithmetic and copies ran while one was open for 18% of the time, Pallas kernels for 0%

profile of v1, /device:TPU:0, one launch (start us, length us, event | category | flops | bytes accessed | tf_op | source)
XLA Modules:
  0.0 3520.8 jit_solution(3230595662735450194)
XLA Ops:
  9.8 59.3 %all-gather.11.cloned.1.call-done = bf16[2048,1024]{1,0:T(8,128)(2,1)} async-done(((bf16[1024,1024]{1,0:T(8,128)(2,1)}), bf16[2048,1024]{1,0:T(8,128)(2,1)}) %all-gather.11.cloned.1.call-update) | async-done | bytes 4194320 | tf_op jit(solution)/shard_map/all_gather | solution.py:132
  108.9 92.2 %while.52 = (s32[]{:T(128)}, bf16[2,1024,4,2,64]{1,4,3,2,0:T(8,128)(2,1)S(1)}, f32[2,4,2,1024]{3,2,1,0:T(2,128)S(1)}, bf16[2,1024,4,64]{1,3,2,0:T(8,128)(2,1)}, ...) while((s32[]{:T(128)}, bf16[2,1024,4,2,64]{1,4,3,2,0:T(8,128)(2,1)S(1)}, ...), condition=%wide.region_4.5_spmd, body=%wide.region_1.4_spmd.sunk | while | flops 2249711616 | bytes 108267600 | solution.py:155
  211.8 98.6 %reduce-scatter.8.cloned.1.call-done = f32[1024,1024]{1,0:T(8,128)} async-done(((f32[2048,1024]{1,0:T(8,128)}), f32[1024,1024]{1,0:T(8,128)}) %reduce-scatter.8.cloned.1.call-update) | async-done | bytes 4194320 | tf_op jit(solution)/shard_map/reduce_scatter | solution.py:158
  317.2 51.7 %all-gather.15.cloned.1.call-done = bf16[2048,1024]{1,0:T(8,128)(2,1)} async-done(((bf16[1024,1024]{1,0:T(8,128)(2,1)}), bf16[2048,1024]{1,0:T(8,128)(2,1)}) %all-gather.15.cloned.1.call-update) | async-done | bytes 4194320 | tf_op jit(solution)/shard_map/all_gather | solution.py:187
  368.9 58.8 %all-gather.13.cloned.1.call-done = bf16[2048,1024]{1,0:T(8,128)(2,1)} async-done(((bf16[1024,1024]{1,0:T(8,128)(2,1)}), bf16[2048,1024]{1,0:T(8,128)(2,1)}) %all-gather.13.cloned.1.call-update) | async-done | bytes 4194320 | tf_op jit(solution)/shard_map/all_gather | solution.py:161
  432.1 819.8 %while.54 = (s32[]{:T(128)}, f32[2048,1024]{1,0:T(8,128)}, bf16[4,8,256,1024]{3,2,1,0:T(8,128)(2,1)}, bf16[4,8,256,1024]{3,2,1,0:T(8,128)(2,1)}, bf16[4,8,256,10...) while((s32[]{:T(128)}, f32[2048,1024]{1,0:T(8,128)}, ...), condition=%wide.region_13.14_spmd, body=%wide.region_11.13_spmd.sunk | while | flops 21541720064 | bytes 387395840 | solution.py:228
  435.1 28.4 gather_fusion.2
  463.5 28.4 gather_fusion.1
  585.6 51.6 %scatter_fusion.1 = f32[2048,1024]{1,0:T(8,128)} fusion(f32[2048,1024]{1,0:T(8,128)} %get-tuple-element.629, s32[5120]{0:T(1024)S(1)} %bitcast.414, f32[5120,1024]{1,0:T(8,128)} %bitcast.390), kind=kCustom, calls=%fused_computation.4.clone.1 | custom fusion | flops 5242880 | bytes 62935040 | tf_op jit(solution)/shard_map/while/body/eval_jaxpr/scatter-add | solution.py:224
  640.0 28.4 gather_fusion.2
  668.4 28.4 gather_fusion.1
  790.3 51.6 %scatter_fusion.1 = f32[2048,1024]{1,0:T(8,128)} fusion(f32[2048,1024]{1,0:T(8,128)} %get-tuple-element.629, s32[5120]{0:T(1024)S(1)} %bitcast.414, f32[5120,1024]{1,0:T(8,128)} %bitcast.390), kind=kCustom, calls=%fused_computation.4.clone.1 | custom fusion | flops 5242880 | bytes 62935040 | tf_op jit(solution)/shard_map/while/body/eval_jaxpr/scatter-add | solution.py:224
  844.8 28.4 gather_fusion.2
  873.2 28.4 gather_fusion.1
  995.2 51.6 %scatter_fusion.1 = f32[2048,1024]{1,0:T(8,128)} fusion(f32[2048,1024]{1,0:T(8,128)} %get-tuple-element.629, s32[5120]{0:T(1024)S(1)} %bitcast.414, f32[5120,1024]{1,0:T(8,128)} %bitcast.390), kind=kCustom, calls=%fused_computation.4.clone.1 | custom fusion | flops 5242880 | bytes 62935040 | tf_op jit(solution)/shard_map/while/body/eval_jaxpr/scatter-add | solution.py:224
  1049.6 28.4 gather_fusion.2
  1078.1 28.4 gather_fusion.1
  1199.9 51.6 %scatter_fusion.1 = f32[2048,1024]{1,0:T(8,128)} fusion(f32[2048,1024]{1,0:T(8,128)} %get-tuple-element.629, s32[5120]{0:T(1024)S(1)} %bitcast.414, f32[5120,1024]{1,0:T(8,128)} %bitcast.390), kind=kCustom, calls=%fused_computation.4.clone.1 | custom fusion | flops 5242880 | bytes 62935040 | tf_op jit(solution)/shard_map/while/body/eval_jaxpr/scatter-add | solution.py:224
  1258.1 54.4 %reduce-scatter.12.cloned.1.call-done = bf16[1024,1024]{1,0:T(8,128)(2,1)} async-done(((bf16[2048,1024]{1,0:T(8,128)(2,1)}), bf16[1024,1024]{1,0:T(8,128)(2,1)}) %reduce-scatter.12.cloned.1.call-update) | async-done | bytes 2097168 | tf_op jit(solution)/shard_map/reduce_scatter | solution.py:258
  1321.6 56.8 %all-gather.17.cloned.1.call-done = bf16[2048,1024]{1,0:T(8,128)(2,1)} async-done(((bf16[1024,1024]{1,0:T(8,128)(2,1)}), bf16[2048,1024]{1,0:T(8,128)(2,1)}) %all-gather.17.cloned.1.call-update) | async-done | bytes 4194320 | tf_op jit(solution)/shard_map/all_gather | solution.py:265
  1397.2 333.4 %while.55 = (s32[]{:T(128)}, f32[2,1024,4,2,64]{1,0,4,3,2:T(2,128)}, f32[2,1024,4,64]{1,0,3,2:T(2,128)}, bf16[2,1024,4,64]{1,3,2,0:T(8,128)(2,1)}, bf16[2,1024,4...) while((s32[]{:T(128)}, ...), condition=%wide.region_18.19_spmd, body=%wide.region_16.18_spmd.sunk | while | flops 5496365056 | bytes 282823840 | solution.py:273
  1455.8 28.1 fusion.241
  1527.3 36.6 %dynamic_update_slice.49 = f32[2,1024,4,2,64]{1,0,4,3,2:T(2,128)} dynamic-update-slice(f32[2,1024,4,2,64]{1,0,4,3,2:T(2,128)} %get-tuple-element.666, f32[1,1024,4,2,64]{1,0,4,3,2:T(1,128)S(1)} %copy.117, s32[]{:T(128)S(6)} %copy.157, s32[]{:T(128)} %constant.124.clone.1..sunk, s32[]{:T(128)} %constant.124.clone.1..sunk, s32[]{:T(128)} %constant.124.clone.1..sunk, s32[]{:T(128)} %constant.124.clone.1..sunk) | dynamic-update-slice | bytes 4194308 | tf_op jit(solution)/shard_map/while/body/jit(dynamic_update_index_in_dim)/dynamic_update_slice | solution.py:273
  1597.5 24.7 fusion.240
  1622.3 28.1 fusion.241
  1693.7 36.6 %dynamic_update_slice.49 = f32[2,1024,4,2,64]{1,0,4,3,2:T(2,128)} dynamic-update-slice(f32[2,1024,4,2,64]{1,0,4,3,2:T(2,128)} %get-tuple-element.666, f32[1,1024,4,2,64]{1,0,4,3,2:T(1,128)S(1)} %copy.117, s32[]{:T(128)S(6)} %copy.157, s32[]{:T(128)} %constant.124.clone.1..sunk, s32[]{:T(128)} %constant.124.clone.1..sunk, s32[]{:T(128)} %constant.124.clone.1..sunk, s32[]{:T(128)} %constant.124.clone.1..sunk) | dynamic-update-slice | bytes 4194308 | tf_op jit(solution)/shard_map/while/body/jit(dynamic_update_index_in_dim)/dynamic_update_slice | solution.py:273
  1768.7 432.4 %while.53 = (s32[]{:T(128)}, f32[2048,1024]{1,0:T(8,128)}, s32[4,8,640]{2,1,0:T(8,128)}, bf16[2048,1024]{1,0:T(8,128)(2,1)}, bf16[4,8,256,1024]{3,2,1,0:T(8,128)...) while((s32[]{:T(128)}, f32[2048,1024]{1,0:T(8,128)}, ...), condition=%wide.region_9.10_spmd, body=%wide.region_7.9_spmd.sunk | while | flops 8071449600 | bytes 149247088 | solution.py:178
  1771.1 28.4 gather_fusion
  1825.4 51.6 %scatter_fusion = f32[2048,1024]{1,0:T(8,128)} fusion(f32[2048,1024]{1,0:T(8,128)} %get-tuple-element.697, s32[5120]{0:T(1024)S(1)} %bitcast.415, f32[5120,1024]{1,0:T(8,128)} %bitcast.391), kind=kCustom, calls=%fused_computation.3.clone.1 | custom fusion | flops 5242880 | bytes 62935040 | tf_op jit(solution)/shard_map/while/body/eval_jaxpr/scatter-add | solution.py:175
  1879.3 28.4 gather_fusion
  1933.4 51.6 %scatter_fusion = f32[2048,1024]{1,0:T(8,128)} fusion(f32[2048,1024]{1,0:T(8,128)} %get-tuple-element.697, s32[5120]{0:T(1024)S(1)} %bitcast.415, f32[5120,1024]{1,0:T(8,128)} %bitcast.391), kind=kCustom, calls=%fused_computation.3.clone.1 | custom fusion | flops 5242880 | bytes 62935040 | tf_op jit(solution)/shard_map/while/body/eval_jaxpr/scatter-add | solution.py:175
  1987.3 28.4 gather_fusion
  2041.4 51.6 %scatter_fusion = f32[2048,1024]{1,0:T(8,128)} fusion(f32[2048,1024]{1,0:T(8,128)} %get-tuple-element.697, s32[5120]{0:T(1024)S(1)} %bitcast.415, f32[5120,1024]{1,0:T(8,128)} %bitcast.391), kind=kCustom, calls=%fused_computation.3.clone.1 | custom fusion | flops 5242880 | bytes 62935040 | tf_op jit(solution)/shard_map/while/body/eval_jaxpr/scatter-add | solution.py:175
  2095.2 28.4 gather_fusion
  2149.5 51.6 %scatter_fusion = f32[2048,1024]{1,0:T(8,128)} fusion(f32[2048,1024]{1,0:T(8,128)} %get-tuple-element.697, s32[5120]{0:T(1024)S(1)} %bitcast.415, f32[5120,1024]{1,0:T(8,128)} %bitcast.391), kind=kCustom, calls=%fused_computation.3.clone.1 | custom fusion | flops 5242880 | bytes 62935040 | tf_op jit(solution)/shard_map/while/body/eval_jaxpr/scatter-add | solution.py:175
  2311.8 132.9 %reduce-scatter.20.cloned.1.call-done = bf16[32,256,64]{1,0,2:T(8,128)(2,1)} async-done(((bf16[32,256,1024]{1,0,2:T(8,128)(2,1)}), bf16[32,256,64]{1,0,2:T(8,128)(2,1)}) %reduce-scatter.20.cloned.1.call-update) | async-done | bytes 1048592 | tf_op jit(solution)/shard_map/reduce_scatter | solution.py:243
  2444.8 182.0 %reduce-scatter.16.cloned.1.call-done = bf16[32,256,64]{1,0,2:T(8,128)(2,1)} async-done(((bf16[32,256,1024]{1,0,2:T(8,128)(2,1)}), bf16[32,256,64]{1,0,2:T(8,128)(2,1)}) %reduce-scatter.16.cloned.1.call-update) | async-done | bytes 1048592 | tf_op jit(solution)/shard_map/reduce_scatter | solution.py:237
  2626.8 182.2 %reduce-scatter.18.cloned.1.call-done = bf16[32,256,64]{1,0,2:T(8,128)(2,1)} async-done(((bf16[32,256,1024]{1,0,2:T(8,128)(2,1)}), bf16[32,256,64]{1,0,2:T(8,128)(2,1)}) %reduce-scatter.18.cloned.1.call-update) | async-done | bytes 1048592 | tf_op jit(solution)/shard_map/reduce_scatter | solution.py:240
  2815.4 31.0 psum.28
  2847.0 64.4 %all-reduce.4.cloned.1.call-done = (bf16[256,1024]{1,0:T(8,128)(2,1)}, bf16[256,1024]{1,0:T(8,128)(2,1)}, bf16[512,1024]{1,0:T(8,128)(2,1)}) async-done(((bf16[256,1024]{1,0:T(8,128)(2,1)}, bf16[256,1024]{1,0:T(8,128)(2,1)}, bf16[512,1024]{1,0:T(8,128)(2,1)}), (bf16[256,1024]{1,0:T(8,128)(2,1)}, bf16[256,1024]{1,0:T(8,128)(2,1)}, bf16[512,1024]{1,0:T(8,128)(2,1)})) %all-reduce.4.cloned.1.call-update) | async-done | bytes 2097168 | tf_op jit(solution)/shard_map/psum | solution.py:308
  2918.4 51.5 %all-gather.19.cloned.1.call-done = bf16[2048,1024]{1,0:T(8,128)(2,1)} async-done(((bf16[1024,1024]{1,0:T(8,128)(2,1)}), bf16[2048,1024]{1,0:T(8,128)(2,1)}) %all-gather.19.cloned.1.call-update) | async-done | bytes 4194320 | tf_op jit(solution)/shard_map/all_gather | solution.py:303
  2969.9 129.7 %all-gather.27.cloned.1.call-done = bf16[16384,512]{1,0:T(8,128)(2,1)} async-done(((bf16[1024,512]{1,0:T(8,128)(2,1)}), bf16[16384,512]{1,0:T(8,128)(2,1)}) %all-gather.27.cloned.1.call-update) | async-done | bytes 16777232 | tf_op jit(solution)/shard_map/all_gather | solution.py:305
  3110.7 116.3 %all-gather.25.cloned.1.call-done = bf16[32,256,1024]{1,0,2:T(8,128)(2,1)} async-done(((bf16[32,256,64]{1,0,2:T(8,128)(2,1)}), bf16[32,256,1024]{1,0,2:T(8,128)(2,1)}) %all-gather.25.cloned.1.call-update) | async-done | bytes 16777232 | tf_op jit(solution)/shard_map/all_gather | solution.py:254
  3227.0 27.7 copy.79
  3254.7 99.5 %all-gather.21.cloned.1.call-done = bf16[32,256,1024]{1,0,2:T(8,128)(2,1)} async-done(((bf16[32,256,64]{1,0,2:T(8,128)(2,1)}), bf16[32,256,1024]{1,0,2:T(8,128)(2,1)}) %all-gather.21.cloned.1.call-update) | async-done | bytes 16777232 | tf_op jit(solution)/shard_map/all_gather | solution.py:248
  3354.2 27.7 copy.77
  3382.0 99.6 %all-gather.23.cloned.1.call-done = bf16[32,256,1024]{1,0,2:T(8,128)(2,1)} async-done(((bf16[32,256,64]{1,0,2:T(8,128)(2,1)}), bf16[32,256,1024]{1,0,2:T(8,128)(2,1)}) %all-gather.23.cloned.1.call-update) | async-done | bytes 16777232 | tf_op jit(solution)/shard_map/all_gather | solution.py:251
  3481.6 27.5 copy.78
  (381 shorter events, 1044.0 us)
Async XLA Ops:
  7.2 198.0 %copy-start = (bf16[512,1024]{1,0:T(8,128)(2,1)S(1)}, bf16[512,1024]{1,0:T(8,128)(2,1)}, u32[]{:S(2)}) copy-start(bf16[512,1024]{1,0:T(8,128)(2,1)} %param.27) | copy-start | bytes 3145732
  7.2 65.1 %copy-start.48 = (f32[1024]{0:T(1024)S(1)}, f32[1024]{0:T(1024)}, u32[]{:S(2)}) copy-start(f32[1024]{0:T(1024)} %param.22) | copy-start | bytes 12292
  7.2 61.9 %all-gather.11.cloned.1.call-start = ((), (), s32[]{:S(2)}) async-start(), calls=%async_computation.7 | async-start | bytes 6291456 | tf_op jit(solution)/shard_map/all_gather | solution.py:132
  7.9 302.5 %reduce-scatter.8.cloned.1.call-start = ((), (), s32[]{:S(2)}) async-start(), calls=%async_computation.8 | async-start | bytes 12582912 | tf_op jit(solution)/shard_map/reduce_scatter | solution.py:158
  9.8 87.9 %copy-start.13 = (f32[2048,32]{0,1:T(8,128)}, f32[2048,32]{0,1:T(8,128)S(1)}, u32[]{:S(2)}) copy-start(f32[2048,32]{0,1:T(8,128)S(1)} %get-tuple-element.361) | copy-start | bytes 786436
  211.0 99.4 %copy-start.10 = (bf16[1024,1024]{1,0:T(8,128)(2,1)S(1)}, bf16[1024,1024]{1,0:T(8,128)(2,1)}, u32[]{:S(2)}) copy-start(bf16[1024,1024]{1,0:T(8,128)(2,1)} %param.21) | copy-start | bytes 6291460
  211.0 157.8 %all-gather.15.cloned.1.call-start = ((), (), s32[]{:S(2)}) async-start(), calls=%async_computation.11 | async-start | bytes 6291456 | tf_op jit(solution)/shard_map/all_gather | solution.py:187
  211.8 103.6 %copy-start.41 = (f32[1024]{0:T(1024)S(1)}, f32[1024]{0:T(1024)}, u32[]{:S(2)}) copy-start(f32[1024]{0:T(1024)} %param.23) | copy-start | bytes 12292
  211.8 215.9 %all-gather.13.cloned.1.call-start = ((), (), s32[]{:S(2)}) async-start(), calls=%async_computation.9 | async-start | bytes 6291456 | tf_op jit(solution)/shard_map/all_gather | solution.py:161
  317.1 995.4 %reduce-scatter.12.cloned.1.call-start = ((), (), s32[]{:S(2)}) async-start(), calls=%async_computation.12 | async-start | bytes 6291456 | tf_op jit(solution)/shard_map/reduce_scatter | solution.py:258
  492.0 10.5 copy-start.2
  535.1 10.4 copy-start.4
  545.5 9.3 copy-start.3
  566.1 19.4 copy-start.29
  696.9 10.5 copy-start.2
  739.9 10.4 copy-start.4
  750.3 9.3 copy-start.3
  770.9 19.4 copy-start.29
  901.6 10.5 copy-start.2
  944.8 10.4 copy-start.4
  955.2 9.3 copy-start.3
  975.7 19.4 copy-start.29
  1106.5 10.5 copy-start.2
  1149.5 10.4 copy-start.4
  1159.9 9.3 copy-start.3
  1180.5 19.4 copy-start.29
  1258.0 54.5 %copy-start.36 = (f32[1024]{0:T(1024)S(1)}, f32[1024]{0:T(1024)}, u32[]{:S(2)}) copy-start(f32[1024]{0:T(1024)} %copy-done.35) | copy-start | bytes 12292
  1258.0 54.5 %copy-start.42 = (f32[1024]{0:T(1024)S(1)}, f32[1024]{0:T(1024)}, u32[]{:S(2)}) copy-start(f32[1024]{0:T(1024)} %param.23) | copy-start | bytes 12292
  1258.0 59.9 %copy-start.12 = (bf16[1024,1024]{1,0:T(8,128)(2,1)S(1)}, bf16[1024,1024]{1,0:T(8,128)(2,1)}, u32[]{:S(2)}) copy-start(bf16[1024,1024]{1,0:T(8,128)(2,1)} %param.33) | copy-start | bytes 6291460
  1258.0 59.9 %copy-start.44 = (f32[1024]{0:T(1024)S(1)}, f32[1024]{0:T(1024)}, u32[]{:S(2)}) copy-start(f32[1024]{0:T(1024)} %get-tuple-element.365) | copy-start | bytes 12292
  1258.0 120.4 %all-gather.17.cloned.1.call-start = ((), (), s32[]{:S(2)}) async-start(), calls=%async_computation.13 | async-start | bytes 6291456 | tf_op jit(solution)/shard_map/all_gather | solution.py:265
  1321.5 974.1 %reduce-scatter.14.cloned.1.call-start = ((), (), s32[]{:S(2)}) async-start(), calls=%async_computation.14 | async-start | bytes 6291456 | tf_op jit(solution)/shard_map/reduce_scatter | solution.py:292
  1386.6 10.6 copy-start.34
  1764.3 533.8 %reduce-scatter.10.cloned.1.call-start = ((), (), s32[]{:S(2)}) async-start(), calls=%async_computation.10 | async-start | bytes 6291456 | tf_op jit(solution)/shard_map/reduce_scatter | solution.py:183
  2207.1 237.6 %reduce-scatter.20.cloned.1.call-start = ((), (), s32[]{:S(2)}) async-start(), calls=%async_computation.20 | async-start | bytes 17825792 | tf_op jit(solution)/shard_map/reduce_scatter | solution.py:243
  2231.3 395.5 %reduce-scatter.16.cloned.1.call-start = ((), (), s32[]{:S(2)}) async-start(), calls=%async_computation.16 | async-start | bytes 17825792 | tf_op jit(solution)/shard_map/reduce_scatter | solution.py:237
  2255.7 553.3 %reduce-scatter.18.cloned.1.call-start = ((), (), s32[]{:S(2)}) async-start(), calls=%async_computation.18 | async-start | bytes 17825792 | tf_op jit(solution)/shard_map/reduce_scatter | solution.py:240
  2280.3 7.7 copy-start.18
  2280.3 631.0 %all-reduce.4.cloned.1.call-start = ((), (), s32[]{:S(2)}) async-start(), calls=%async_computation.23 | async-start | bytes 4194304 | tf_op jit(solution)/shard_map/psum | solution.py:308
  2281.0 7.0 copy-start.22
  2295.6 674.3 %all-gather.19.cloned.1.call-start = ((), (), s32[]{:S(2)}) async-start(), calls=%async_computation.15 | async-start | bytes 6291456 | tf_op jit(solution)/shard_map/all_gather | solution.py:303
  2305.4 794.2 %all-gather.27.cloned.1.call-start = ((), (), s32[]{:S(2)}) async-start(), calls=%async_computation.22 | async-start | bytes 17825792 | tf_op jit(solution)/shard_map/all_gather | solution.py:305
  2311.7 497.4 %copy-start.55 = (u32[32]{0:T(128)S(1)}, u32[32]{0:T(128)}, u32[]{:S(2)}) copy-start(u32[32]{0:T(128)} %constant.139) | copy-start | bytes 388
  2311.7 498.0 %copy-start.50 = (bf16[1024]{0:T(1024)(128)(2,1)S(1)}, bf16[1024]{0:T(1024)(128)(2,1)}, u32[]{:S(2)}) copy-start(bf16[1024]{0:T(1024)(128)(2,1)} %get-tuple-element.266) | copy-start | bytes 6148
  2311.7 498.0 %copy-start.51 = (bf16[1024]{0:T(1024)(128)(2,1)S(1)}, bf16[1024]{0:T(1024)(128)(2,1)}, u32[]{:S(2)}) copy-start(bf16[1024]{0:T(1024)(128)(2,1)} %get-tuple-element.349) | copy-start | bytes 6148
  2311.7 915.3 %all-gather.25.cloned.1.call-start = ((), (), s32[]{:S(2)}) async-start(), calls=%async_computation.21 | async-start | bytes 17825792 | tf_op jit(solution)/shard_map/all_gather | solution.py:254
  2444.7 909.5 %all-gather.21.cloned.1.call-start = ((), (), s32[]{:S(2)}) async-start(), calls=%async_computation.17 | async-start | bytes 17825792 | tf_op jit(solution)/shard_map/all_gather | solution.py:248
  2626.8 854.8 %all-gather.23.cloned.1.call-start = ((), (), s32[]{:S(2)}) async-start(), calls=%async_computation.19 | async-start | bytes 17825792 | tf_op jit(solution)/shard_map/all_gather | solution.py:251
  (38 other events, 120.0 us)
Sparse Core Ops, SparseCore 0:
  9.6 59.4 all-gather.10
  211.2 99.2 reduce-scatter.7
  312.1 56.7 all-gather.14
  370.9 56.7 all-gather.12
  1258.1 54.3 reduce-scatter.11
  1321.7 56.7 all-gather.16
  1764.4 54.2 reduce-scatter.13
  2207.2 54.7 reduce-scatter.9
  2266.1 178.5 reduce-scatter.19
  2449.2 177.5 reduce-scatter.15
  2631.5 177.5 reduce-scatter.17
  2813.9 97.3 all-reduce.3
  2913.5 56.2 all-gather.18
  2972.7 126.8 all-gather.26
  3101.9 125.0 all-gather.24
  3229.2 124.9 all-gather.20
  3356.5 125.0 all-gather.22
